TPU v7x, 32 devices: a whole 2x2x4 slice. The times are simulated.
32 devices in a mesh: row: 8 (over z, core), col: 4 (over y, x).
Axes of the slice: x: 2, y: 2, z: 4, core: 2. Of those that a mesh axis runs over, the one named last changes fastest.
Arguments:
- gram: bfloat16 [32768, 32768], P('row', 'col'), may hold values from -1 to 5, as said below
- start_basis: bfloat16 [32768, 256], P(('row', 'col')), may hold values from -12 to 12
- slab: float32 [32768, 4096], P('row', 'col'), may hold values from -6 to 6
Outputs:
- core_scaled: float32 [32768, 256], P(('row', 'col'))
- next_unfolding: float32 [4096, 256], P(('row', 'col'))
Inputs may be any that keep to these rules, and one draw needn't show every extreme that they name: gram is symmetric: entry (i, j) equals entry (j, i).
All inputs are finite; a program needn't handle non-finite values.
Results may differ from a plain program's by a relative error of at most 0.003.
Values may be sent and summed in bfloat16 or wider, within the bound.
A program may use at most 192 MiB of HBM per device.

v0:
```python
import math
import jax
import jax.numpy as jnp
from jax import lax
from jax.sharding import PartitionSpec as P

N = 32768
NMODE = 16


def body(gram, start_basis, slab):
    col_count = lax.axis_size("col")
    highest = lax.Precision.HIGHEST
    contract_rows = (((0,), (0,)), ((), ()))
    own_rows = lax.all_gather(start_basis, "col", axis=0, tiled=True)
    first_image = lax.psum_scatter(
        lax.dot_general(gram, own_rows, contract_rows, preferred_element_type=jnp.float32),
        "row",
        scatter_dimension=0,
        tiled=True,
    ).astype(jnp.bfloat16)
    col_rows = lax.all_gather(first_image, "row", axis=0, tiled=True)
    second_image = lax.psum_scatter(
        jnp.dot(gram, col_rows, preferred_element_type=jnp.float32),
        "col",
        scatter_dimension=0,
        tiled=True,
    )
    own_gram = lax.dot_general(
        second_image,
        second_image,
        contract_rows,
        precision=highest,
        preferred_element_type=jnp.float32,
    )
    small_gram = lax.psum(own_gram, ("row", "col"))
    factor = jnp.linalg.cholesky(small_gram)
    basis_cols = jax.scipy.linalg.solve_triangular(factor, second_image.T, lower=True).T
    block_basis = lax.all_gather(basis_cols, "col", axis=0, tiled=True)
    own_proj = lax.psum_scatter(
        lax.dot_general(
            block_basis, slab, contract_rows, precision=highest, preferred_element_type=jnp.float32
        ),
        "row",
        scatter_dimension=0,
        tiled=True,
    )
    core_out = basis_cols * math.sqrt(N)
    mode_share = NMODE // col_count
    grouped = own_proj.reshape(own_proj.shape[0], mode_share, own_proj.shape[1] // mode_share)
    regrouped = lax.all_to_all(grouped, "col", split_axis=0, concat_axis=1, tiled=True)
    return (
        core_out,
        regrouped.reshape(regrouped.shape[0] * regrouped.shape[1], regrouped.shape[2]),
    )


def solution(mesh):
    in_specs = (P("row", "col"), P(("row", "col"), None), P("row", "col"))
    out_specs = (P(("row", "col"), None), P(("row", "col"), None))
    return jax.shard_map(body, mesh=mesh, in_specs=in_specs, out_specs=out_specs, check_vma=False)
```

profile of v0, /device:TPU:0, one launch (start us, length us, event | category | flops | bytes accessed | tf_op | source)
XLA Modules:
  0.0 614.0 jit_solution(10611750755675535246)
XLA Ops:
  7.2 0.0 all-gather.4.cloned.1.call-start
  7.2 0.7 all-gather.4.cloned.1.call-update
  7.9 0.0 reduce-scatter.4.cloned.1.call-start
  7.9 39.8 %all-gather.4.cloned.1.call-done = bf16[4096,256]{1,0:T(8,128)(2,1)} async-done(((bf16[1024,256]{1,0:T(8,128)(2,1)}), bf16[4096,256]{1,0:T(8,128)(2,1)}) %all-gather.4.cloned.1.call-update) | async-done | bytes 2097168 | tf_op jit(solution)/shard_map/all_gather | solution.py:15
  47.8 30.0 %fusion.9 = f32[8192,256]{1,0:T(8,128)} fusion(bf16[4096,8192]{1,0:T(8,128)(2,1)} %param.3, bf16[4096,256]{1,0:T(8,128)(2,1)} %all-gather.4.cloned.1.call-done), kind=kOutput, calls=%fused_computation.32 | convolution fusion | flops 17179869184 | bytes 77594624 | tf_op jit(solution)/shard_map/dot_general | solution.py:17
  77.7 0.0 reduce-scatter.4.cloned.1.call-update
  77.7 0.0 all-gather.6.cloned.1.call-start
  77.8 89.6 %reduce-scatter.4.cloned.1.call-done = f32[1024,256]{1,0:T(8,128)} async-done(((f32[8192,256]{1,0:T(8,128)}), f32[1024,256]{1,0:T(8,128)}) %reduce-scatter.4.cloned.1.call-update) | async-done | bytes 1048592 | tf_op jit(solution)/shard_map/reduce_scatter | solution.py:16
  167.4 2.1 convert_element_type.3
  169.5 0.0 all-gather.6.cloned.1.call-update
  169.5 0.0 reduce-scatter.6.cloned.1.call-start
  169.6 45.4 %all-gather.6.cloned.1.call-done = bf16[8192,256]{1,0:T(8,128)(2,1)} async-done(((bf16[1024,256]{1,0:T(8,128)(2,1)}), bf16[8192,256]{1,0:T(8,128)(2,1)}) %all-gather.6.cloned.1.call-update) | async-done | bytes 4194320 | tf_op jit(solution)/shard_map/all_gather | solution.py:22
  215.0 29.2 %convolution_bitcast_fusion = f32[4096,256]{0,1:T(8,128)} fusion(bf16[8192,256]{1,0:T(8,128)(2,1)} %all-gather.6.cloned.1.call-done, bf16[4096,8192]{1,0:T(8,128)(2,1)} %param.3), kind=kOutput, calls=%fused_computation.2 | convolution fusion | flops 17179869184 | bytes 75497472 | tf_op jit(solution)/shard_map/dot_general | solution.py:24
  244.2 0.0 reduce-scatter.6.cloned.1.call-update
  244.2 0.0 all-reduce.3.cloned.1.call-start
  244.3 51.5 %reduce-scatter.6.cloned.1.call-done = f32[1024,256]{0,1:T(8,128)} async-done(((f32[4096,256]{0,1:T(8,128)}), f32[1024,256]{0,1:T(8,128)}) %reduce-scatter.6.cloned.1.call-update) | async-done | bytes 1048592 | tf_op jit(solution)/shard_map/reduce_scatter | solution.py:23
  295.8 0.0 copy-start
  295.8 3.4 fusion.10
  299.1 0.0 all-reduce.3.cloned.1.call-update
  299.1 0.2 all-gather.8.cloned.1.call-start
  299.4 128.9 %all-reduce.3.cloned.1.call-done = f32[256,256]{0,1:T(8,128)} async-done(((f32[256,256]{0,1:T(8,128)}), f32[256,256]{0,1:T(8,128)}) %all-reduce.3.cloned.1.call-update) | async-done | bytes 262160 | tf_op jit(solution)/shard_map/psum | solution.py:36
  428.3 1.1 copy.6
  429.4 1.0 fusion.2
  430.4 11.7 %cholesky.50 = f32[128,128]{1,0:T(8,128)S(1)} custom-call(f32[128,128]{1,0:T(8,128)S(1)} %cholesky.118), custom_call_target="Cholesky" | custom-call | tf_op jit(solution)/shard_map/jit(cholesky)/cholesky | solution.py:37
  442.1 9.8 %custom-call.15 = f32[1,128,128]{1,2,0:T(8,128)S(1)} custom-call(f32[1,128,128]{2,1,0:T(8,128)S(1)} %get-tuple-element.25), custom_call_target="InvertDiagBlocksLowerTriangular" | custom-call | tf_op jit(solution)/shard_map/jit(cholesky)/cholesky | solution.py:37
  452.0 0.2 constant_dynamic-update-slice_fusion.1
  452.2 0.3 convolution_subtract_fusion.1
  452.4 11.7 %cholesky.105 = f32[128,128]{1,0:T(8,128)S(1)} custom-call(f32[128,128]{1,0:T(8,128)S(1)} %convolution_subtract_fusion.1), custom_call_target="Cholesky" | custom-call | tf_op jit(solution)/shard_map/jit(cholesky)/cholesky | solution.py:37
  464.2 0.7 compare_reduce_fusion
  466.3 0.1 triangular_solve.57
  466.4 4.3 while.1
  466.6 0.6 fusion.25
  467.1 1.4 bitcast_dynamic-update-slice_fusion.2
  468.6 0.6 fusion.25
  469.2 1.4 bitcast_dynamic-update-slice_fusion.2
  470.6 19.7 %custom-call.16 = f32[2,128,128]{1,2,0:T(8,128)S(1)} custom-call(f32[2,128,128]{2,1,0:T(8,128)S(1)} %get-tuple-element.9), custom_call_target="InvertDiagBlocksLowerTriangular" | custom-call | tf_op jit(solution)/shard_map/jit(_solve_triangular)/triangular_solve | solution.py:38
  490.3 0.0 copy-done
  490.3 0.6 fusion
  491.0 0.6 convolution_subtract_fusion
  491.6 0.6 fusion.4
  492.2 1.0 maximum_bitcast_fusion
  493.2 0.0 all-gather.8.cloned.1.call-update
  493.3 0.0 reduce-scatter.8.cloned.1.call-start
  493.3 51.7 %all-gather.8.cloned.1.call-done = f32[4096,256]{0,1:T(8,128)} async-done(((f32[1024,256]{0,1:T(8,128)}), f32[4096,256]{0,1:T(8,128)}) %all-gather.8.cloned.1.call-update) | async-done | bytes 4194320 | tf_op jit(solution)/shard_map/all_gather | solution.py:39
  545.1 18.3 %fusion.11 = f32[256,1024]{1,0:T(8,128)} fusion(f32[4096,256]{0,1:T(8,128)} %all-gather.8.cloned.1.call-done, f32[4096,1024]{1,0:T(8,128)} %param.5), kind=kOutput, calls=%fused_computation.34 | convolution fusion | flops 12884901888 | bytes 22020096 | tf_op jit(solution)/shard_map/dot_general | solution.py:41
  563.3 0.0 reduce-scatter.8.cloned.1.call-update
  563.3 32.8 %reduce-scatter.8.cloned.1.call-done = f32[32,1024]{1,0:T(8,128)} async-done(((f32[256,1024]{1,0:T(8,128)}), f32[32,1024]{1,0:T(8,128)}) %reduce-scatter.8.cloned.1.call-update) | async-done | bytes 131088 | tf_op jit(solution)/shard_map/reduce_scatter | solution.py:40
  596.1 1.6 reshape.30
  597.7 3.7 all-to-all-start
  601.4 0.1 broadcast_multiply_fusion
  601.5 1.3 copy.8
  602.9 3.6 all-to-all-done
  606.4 0.7 reshape.31
  (10 shorter events, 0.2 us)
Async XLA Ops:
  7.2 40.6 %all-gather.4.cloned.1.call-start = ((), (), s32[]{:S(2)}) async-start(), calls=%async_computation.4 | async-start | bytes 2621440 | tf_op jit(solution)/shard_map/all_gather | solution.py:15
  7.9 159.5 %reduce-scatter.4.cloned.1.call-start = ((), (), s32[]{:S(2)}) async-start(), calls=%async_computation.5 | async-start | bytes 9437184 | tf_op jit(solution)/shard_map/reduce_scatter | solution.py:16
  77.7 137.3 %all-gather.6.cloned.1.call-start = ((), (), s32[]{:S(2)}) async-start(), calls=%async_computation.6 | async-start | bytes 4718592 | tf_op jit(solution)/shard_map/all_gather | solution.py:22
  169.5 126.2 %reduce-scatter.6.cloned.1.call-start = ((), (), s32[]{:S(2)}) async-start(), calls=%async_computation.7 | async-start | bytes 5242880 | tf_op jit(solution)/shard_map/reduce_scatter | solution.py:23
  244.2 184.1 %all-reduce.3.cloned.1.call-start = ((), (), s32[]{:S(2)}) async-start(), calls=%async_computation.8 | async-start | bytes 524288 | tf_op jit(solution)/shard_map/psum | solution.py:36
  295.8 194.6 %copy-start = (f32[1024,256]{0,1:T(8,128)S(1)}, f32[1024,256]{0,1:T(8,128)}, u32[]{:S(2)}) copy-start(f32[1024,256]{0,1:T(8,128)} %reduce-scatter.6.cloned.1.call-done) | copy-start | bytes 3145732
  299.1 245.9 %all-gather.8.cloned.1.call-start = ((), (), s32[]{:S(2)}) async-start(), calls=%async_computation.9 | async-start | bytes 5242880 | tf_op jit(solution)/shard_map/all_gather | solution.py:39
  493.3 102.9 %reduce-scatter.8.cloned.1.call-start = ((), (), s32[]{:S(2)}) async-start(), calls=%async_computation.10 | async-start | bytes 1179648 | tf_op jit(solution)/shard_map/reduce_scatter | solution.py:40
  597.7 8.7 %all-to-all-start = ((f32[32,4,256]{2,1,0:T(4,128)}), f32[32,4,256]{2,1,0:T(4,128)S(1)}, u32[]{:S(2)}, u32[]{:S(2)}) async-start(f32[32,4,256]{2,1,0:T(4,128)} %reshape.30), calls=%async_computation.3 | async-start | bytes 262144 | tf_op jit(solution)/shard_map/all_to_all | solution.py:51
Sparse Core Ops, SparseCore 0:
  9.8 37.8 all-gather.3
  77.9 89.5 reduce-scatter.3
  169.6 45.3 all-gather.5
  244.3 51.3 reduce-scatter.5
  301.7 126.5 all-reduce.2
  493.4 51.6 all-gather.7
  563.5 32.6 reduce-scatter.7
where the time goes:
time: 614 us
  waiting for transfers between devices  444 us (72%)
  matrix products  83.1 us (14%)
  other arithmetic  58 us (9%)
  between operations  15.6 us (3%)
  local copies, waits for them, and re-layouts  8.87 us (1%)
    psum x1, waiting for transfers between devices, body(): small_gram = lax.psum(own_gram, ('row', 'col'))  129 us
    reduce_scatter x1, waiting for transfers between devices, body(): lax.psum_scatter(lax.dot_general(gram, own_rows, contract_rows, preferred...  89.6 us
    all_gather x1, waiting for transfers between devices, body(): block_basis = lax.all_gather(basis_cols, 'col', axis=0, tiled=True)  51.7 us
    reduce_scatter x1, waiting for transfers between devices, body(): lax.psum_scatter(jnp.dot(gram, col_rows, preferred_element_type=jnp.float...  51.5 us
    all_gather x1, waiting for transfers between devices, body(): col_rows = lax.all_gather(first_image, 'row', axis=0, tiled=True)  45.4 us
    all_gather x1, waiting for transfers between devices, body(): own_rows = lax.all_gather(start_basis, 'col', axis=0, tiled=True)  39.8 us
    another operation x6, other arithmetic, body(): factor = jnp.linalg.cholesky(small_gram)  34 us
    reduce_scatter x1, waiting for transfers between devices, body(): lax.psum_scatter(lax.dot_general(block_basis, slab, contract_rows, precis...  32.8 us
  transfers between devices with their start and end apart: 8, of which 8 were waited for; matrix products, arithmetic and copies ran while one was open for 0% of the time, Pallas kernels for 0%

commit v1 on v0

--- a/solution.py
+++ b/solution.py
@@ -36,7 +36,12 @@
     small_gram = lax.psum(own_gram, ("row", "col"))
     factor = jnp.linalg.cholesky(small_gram)
     basis_cols = jax.scipy.linalg.solve_triangular(factor, second_image.T, lower=True).T
-    block_basis = lax.all_gather(basis_cols, "col", axis=0, tiled=True)
+    ring = [basis_cols]
+    for hop in range(3):
+        ring.append(lax.ppermute(ring[-1], "col", [(dev, (dev + 1) % 4) for dev in range(4)]))
+    block_basis = jnp.roll(
+        jnp.concatenate(ring[::-1], axis=0), (lax.axis_index("col") + 1) * ring[0].shape[0], axis=0
+    )
     own_proj = lax.psum_scatter(
         lax.dot_general(
             block_basis, slab, contract_rows, precision=highest, preferred_element_type=jnp.float32

time: 614 us -> 636 us (1.036)
  waiting for transfers between devices: 444 us -> 460 us
    ppermute x0 -> x3, waiting for transfers between devices: none -> 70.5 us  [body(): lax.ppermute(ring[-1], 'col', [(dev, (dev + 1) % 4) for dev in range(4)])]
    all_gather x1 -> x0, waiting for transfers between devices: 51.7 us -> none  [body(): block_basis = lax.all_gather(basis_cols, 'col', axis=0, tiled=True)]
  transfers between devices with their start and end apart: 8 -> 10, of which waited for: 8 -> 10; matrix products, arithmetic and copies ran while one was open for 0% -> 0% of each run, Pallas kernels for 0% -> 0%
where the time goes in v1:
time: 636 us
  waiting for transfers between devices  460 us (72%)
  matrix products  84.2 us (13%)
  other arithmetic  57.3 us (9%)
  between operations  15.6 us (2%)
  local copies, waits for them, and re-layouts  11.9 us (2%)
    psum x1, waiting for transfers between devices, body(): small_gram = lax.psum(own_gram, ('row', 'col'))  129 us
    reduce_scatter x1, waiting for transfers between devices, body(): lax.psum_scatter(lax.dot_general(gram, own_rows, contract_rows, preferred...  89.6 us
    ppermute x3, waiting for transfers between devices, body(): lax.ppermute(ring[-1], 'col', [(dev, (dev + 1) % 4) for dev in range(4)])  70.5 us
    reduce_scatter x1, waiting for transfers between devices, body(): lax.psum_scatter(jnp.dot(gram, col_rows, preferred_element_type=jnp.float...  51.5 us
    all_gather x1, waiting for transfers between devices, body(): col_rows = lax.all_gather(first_image, 'row', axis=0, tiled=True)  45.4 us
    all_gather x1, waiting for transfers between devices, body(): own_rows = lax.all_gather(start_basis, 'col', axis=0, tiled=True)  39.8 us
    another operation x6, other arithmetic, body(): factor = jnp.linalg.cholesky(small_gram)  34 us
    reduce_scatter x1, waiting for transfers between devices, body(): lax.psum_scatter(lax.dot_general(block_basis, slab, contract_rows, precis...  30 us
  transfers between devices with their start and end apart: 10, of which 10 were waited for; matrix products, arithmetic and copies ran while one was open for 0% of the time, Pallas kernels for 0%

profile of v1, /device:TPU:0, one launch (start us, length us, event | category | flops | bytes accessed | tf_op | source)
XLA Modules:
  0.0 635.6 jit_solution(4162626087289670230)
XLA Ops:
  7.2 0.0 all-gather.3.cloned.1.call-start
  7.2 0.7 all-gather.3.cloned.1.call-update
  7.9 0.0 reduce-scatter.4.cloned.1.call-start
  7.9 39.8 %all-gather.3.cloned.1.call-done = bf16[4096,256]{1,0:T(8,128)(2,1)} async-done(((bf16[1024,256]{1,0:T(8,128)(2,1)}), bf16[4096,256]{1,0:T(8,128)(2,1)}) %all-gather.3.cloned.1.call-update) | async-done | bytes 2097168 | tf_op jit(solution)/shard_map/all_gather | solution.py:15
  47.8 30.0 %fusion.12 = f32[8192,256]{1,0:T(8,128)} fusion(bf16[4096,8192]{1,0:T(8,128)(2,1)} %param.3, bf16[4096,256]{1,0:T(8,128)(2,1)} %all-gather.3.cloned.1.call-done), kind=kOutput, calls=%fused_computation.43 | convolution fusion | flops 17179869184 | bytes 77594624 | tf_op jit(solution)/shard_map/dot_general | solution.py:17
  77.7 0.0 reduce-scatter.4.cloned.1.call-update
  77.7 0.0 all-gather.5.cloned.1.call-start
  77.8 89.6 %reduce-scatter.4.cloned.1.call-done = f32[1024,256]{1,0:T(8,128)} async-done(((f32[8192,256]{1,0:T(8,128)}), f32[1024,256]{1,0:T(8,128)}) %reduce-scatter.4.cloned.1.call-update) | async-done | bytes 1048592 | tf_op jit(solution)/shard_map/reduce_scatter | solution.py:16
  167.4 2.1 convert_element_type.3
  169.5 0.0 all-gather.5.cloned.1.call-update
  169.5 0.0 reduce-scatter.6.cloned.1.call-start
  169.6 45.4 %all-gather.5.cloned.1.call-done = bf16[8192,256]{1,0:T(8,128)(2,1)} async-done(((bf16[1024,256]{1,0:T(8,128)(2,1)}), bf16[8192,256]{1,0:T(8,128)(2,1)}) %all-gather.5.cloned.1.call-update) | async-done | bytes 4194320 | tf_op jit(solution)/shard_map/all_gather | solution.py:22
  215.0 29.2 %convolution_bitcast_fusion = f32[4096,256]{0,1:T(8,128)} fusion(bf16[8192,256]{1,0:T(8,128)(2,1)} %all-gather.5.cloned.1.call-done, bf16[4096,8192]{1,0:T(8,128)(2,1)} %param.3), kind=kOutput, calls=%fused_computation.2 | convolution fusion | flops 17179869184 | bytes 75497472 | tf_op jit(solution)/shard_map/dot_general | solution.py:24
  244.2 0.0 reduce-scatter.6.cloned.1.call-update
  244.2 0.0 all-reduce.3.cloned.1.call-start
  244.3 51.5 %reduce-scatter.6.cloned.1.call-done = f32[1024,256]{0,1:T(8,128)} async-done(((f32[4096,256]{0,1:T(8,128)}), f32[1024,256]{0,1:T(8,128)}) %reduce-scatter.6.cloned.1.call-update) | async-done | bytes 1048592 | tf_op jit(solution)/shard_map/reduce_scatter | solution.py:23
  295.8 3.3 fusion.13
  299.0 0.0 all-reduce.3.cloned.1.call-update
  299.1 0.2 reduce-scatter.8.cloned.1.call-start
  299.3 129.0 %all-reduce.3.cloned.1.call-done = f32[256,256]{0,1:T(8,128)} async-done(((f32[256,256]{0,1:T(8,128)}), f32[256,256]{0,1:T(8,128)}) %all-reduce.3.cloned.1.call-update) | async-done | bytes 262160 | tf_op jit(solution)/shard_map/psum | solution.py:36
  428.3 1.1 copy.6
  429.4 1.0 fusion.4
  430.4 11.7 %cholesky.50 = f32[128,128]{1,0:T(8,128)S(1)} custom-call(f32[128,128]{1,0:T(8,128)S(1)} %cholesky.118), custom_call_target="Cholesky" | custom-call | tf_op jit(solution)/shard_map/jit(cholesky)/cholesky | solution.py:37
  442.1 9.8 %custom-call.15 = f32[1,128,128]{1,2,0:T(8,128)S(1)} custom-call(f32[1,128,128]{2,1,0:T(8,128)S(1)} %get-tuple-element.27), custom_call_target="InvertDiagBlocksLowerTriangular" | custom-call | tf_op jit(solution)/shard_map/jit(cholesky)/cholesky | solution.py:37
  452.0 0.2 constant_dynamic-update-slice_fusion.8
  452.2 0.3 convolution_subtract_fusion.1
  452.4 11.7 %cholesky.105 = f32[128,128]{1,0:T(8,128)S(1)} custom-call(f32[128,128]{1,0:T(8,128)S(1)} %convolution_subtract_fusion.1), custom_call_target="Cholesky" | custom-call | tf_op jit(solution)/shard_map/jit(cholesky)/cholesky | solution.py:37
  464.2 0.7 compare_reduce_fusion
  466.3 0.1 triangular_solve.57
  466.4 4.3 while.1
  466.6 0.6 fusion.26
  467.1 1.4 bitcast_dynamic-update-slice_fusion.2
  468.6 0.6 fusion.26
  469.2 1.4 bitcast_dynamic-update-slice_fusion.2
  470.6 19.7 %custom-call.16 = f32[2,128,128]{1,2,0:T(8,128)S(1)} custom-call(f32[2,128,128]{2,1,0:T(8,128)S(1)} %get-tuple-element.9), custom_call_target="InvertDiagBlocksLowerTriangular" | custom-call | tf_op jit(solution)/shard_map/jit(_solve_triangular)/triangular_solve | solution.py:38
  490.3 1.7 fusion.2
  492.0 1.6 convolution_subtract_fusion
  493.6 0.6 fusion.6
  494.3 0.1 maximum_bitcast_fusion
  494.4 1.5 collective-permute-start
  495.9 23.5 %collective-permute-done = f32[1024,256]{0,1:T(8,128)S(1)} collective-permute-done((f32[1024,256]{0,1:T(8,128)S(1)}, f32[1024,256]{0,1:T(8,128)S(1)}, u32[]{:S(2)}, u32[]{:S(2)}) %collective-permute-start) | collective-permute-done | bytes 1048608 | tf_op jit(solution)/shard_map/ppermute | solution.py:41
  519.4 0.6 collective-permute-start.1
  520.0 23.6 %collective-permute-done.1 = f32[1024,256]{0,1:T(8,128)S(1)} collective-permute-done((f32[1024,256]{0,1:T(8,128)S(1)}, f32[1024,256]{0,1:T(8,128)S(1)}, u32[]{:S(2)}, u32[]{:S(2)}) %collective-permute-start.1) | collective-permute-done | bytes 1048608 | tf_op jit(solution)/shard_map/ppermute | solution.py:41
  543.6 0.0 collective-permute-start.2
  543.6 23.4 %collective-permute-done.2 = f32[1024,256]{0,1:T(8,128)} collective-permute-done((f32[1024,256]{0,1:T(8,128)S(1)}, f32[1024,256]{0,1:T(8,128)}, u32[]{:S(2)}, u32[]{:S(2)}) %collective-permute-start.2) | collective-permute-done | bytes 1048608 | tf_op jit(solution)/shard_map/ppermute | solution.py:41
  567.0 1.3 constant_dynamic-update-slice_fusion.7
  568.3 0.1 constant_dynamic-update-slice_fusion.6
  568.4 0.1 constant_dynamic-update-slice_fusion.5
  568.5 0.1 constant_dynamic-update-slice_fusion.4
  568.6 1.3 constant_dynamic-update-slice_fusion.3
  569.9 0.1 constant_dynamic-update-slice_fusion.2
  570.0 0.1 constant_dynamic-update-slice_fusion.1
  570.2 0.3 constant_dynamic-update-slice_fusion
  570.4 17.4 %fusion = f32[256,1024]{1,0:T(8,128)} fusion(f32[4096,1024]{1,0:T(8,128)} %param.5, f32[8192,256]{0,1:T(8,128)S(1)} %get-tuple-element.22, s32[]{:T(128)S(6)} %select_n.19), kind=kOutput, calls=%fused_computation.3 | convolution fusion | flops 12884901888 | bytes 22020100 | tf_op jit(solution)/shard_map/dot_general | solution.py:46
  587.8 0.0 reduce-scatter.8.cloned.1.call-update
  587.8 30.0 %reduce-scatter.8.cloned.1.call-done = f32[32,1024]{1,0:T(8,128)} async-done(((f32[256,1024]{1,0:T(8,128)}), f32[32,1024]{1,0:T(8,128)}) %reduce-scatter.8.cloned.1.call-update) | async-done | bytes 131088 | tf_op jit(solution)/shard_map/reduce_scatter | solution.py:45
  617.8 1.6 reshape.30
  619.5 3.5 all-to-all-start
  623.0 1.3 copy.8
  624.3 3.7 all-to-all-done
  628.0 0.7 reshape.31
  (10 shorter events, 0.2 us)
Async XLA Ops:
  7.2 40.6 %all-gather.3.cloned.1.call-start = ((), (), s32[]{:S(2)}) async-start(), calls=%async_computation.4 | async-start | bytes 2621440 | tf_op jit(solution)/shard_map/all_gather | solution.py:15
  7.9 159.5 %reduce-scatter.4.cloned.1.call-start = ((), (), s32[]{:S(2)}) async-start(), calls=%async_computation.5 | async-start | bytes 9437184 | tf_op jit(solution)/shard_map/reduce_scatter | solution.py:16
  77.7 137.3 %all-gather.5.cloned.1.call-start = ((), (), s32[]{:S(2)}) async-start(), calls=%async_computation.6 | async-start | bytes 4718592 | tf_op jit(solution)/shard_map/all_gather | solution.py:22
  169.5 126.2 %reduce-scatter.6.cloned.1.call-start = ((), (), s32[]{:S(2)}) async-start(), calls=%async_computation.7 | async-start | bytes 5242880 | tf_op jit(solution)/shard_map/reduce_scatter | solution.py:23
  244.2 184.1 %all-reduce.3.cloned.1.call-start = ((), (), s32[]{:S(2)}) async-start(), calls=%async_computation.8 | async-start | bytes 524288 | tf_op jit(solution)/shard_map/psum | solution.py:36
  299.1 318.8 %reduce-scatter.8.cloned.1.call-start = ((), (), s32[]{:S(2)}) async-start(), calls=%async_computation.9 | async-start | bytes 1179648 | tf_op jit(solution)/shard_map/reduce_scatter | solution.py:45
  494.4 25.1 %collective-permute-start = (f32[1024,256]{0,1:T(8,128)S(1)}, f32[1024,256]{0,1:T(8,128)S(1)}, u32[]{:S(2)}, u32[]{:S(2)}) collective-permute-start(f32[1024,256]{0,1:T(8,128)S(1)} %maximum_bitcast_fusion), channel_id=1, source_target_pairs={{0,1},{1,2},{2,3},{3,0},{4,5},{5,6},{6,7},{7,4},{8,9},{9,10},{10,1... | collective-permute-start | bytes 3145736 | tf_op jit(solution)/shard_map/ppermute | solution.py:41
  519.4 24.1 %collective-permute-start.1 = (f32[1024,256]{0,1:T(8,128)S(1)}, f32[1024,256]{0,1:T(8,128)S(1)}, u32[]{:S(2)}, u32[]{:S(2)}) collective-permute-start(f32[1024,256]{0,1:T(8,128)S(1)} %collective-permute-done), channel_id=1, source_target_pairs={{0,1},{1,2},{2,3},{3,0},{4,5},{5,6},{6,7},{7,4},{8,9},{9,10},{10,1... | collective-permute-start | bytes 3145736 | tf_op jit(solution)/shard_map/ppermute | solution.py:41
  543.6 23.4 %collective-permute-start.2 = (f32[1024,256]{0,1:T(8,128)S(1)}, f32[1024,256]{0,1:T(8,128)}, u32[]{:S(2)}, u32[]{:S(2)}) collective-permute-start(f32[1024,256]{0,1:T(8,128)S(1)} %collective-permute-done.1), channel_id=1, source_target_pairs={{0,1},{1,2},{2,3},{3,0},{4,5},{5,6},{6,7},{7,4},{8,9},{9,10},{10,1... | collective-permute-start | bytes 3145736 | tf_op jit(solution)/shard_map/ppermute | solution.py:41
  619.5 8.6 %all-to-all-start = ((f32[32,4,256]{2,1,0:T(4,128)}), f32[32,4,256]{2,1,0:T(4,128)S(1)}, u32[]{:S(2)}, u32[]{:S(2)}) async-start(f32[32,4,256]{2,1,0:T(4,128)} %reshape.30), calls=%async_computation.3 | async-start | bytes 262144 | tf_op jit(solution)/shard_map/all_to_all | solution.py:56
Sparse Core Ops, SparseCore 0:
  9.8 37.8 all-gather.2
  77.9 89.5 reduce-scatter.3
  169.6 45.3 all-gather.4
  244.3 51.3 reduce-scatter.5
  301.7 126.5 all-reduce.2
  587.9 29.8 reduce-scatter.7
